TPU v7x, 256 devices: a whole 4x4x8 slice. The times are simulated.
256 devices in a mesh: ctx: 8 (over x, y_lo), chan: 32 (over y_hi, z, core).
Axes of the slice: x: 4, y: 4 (y_hi: 2, y_lo: 2; y = y_hi * 2 + y_lo), z: 8, core: 2. Of those that a mesh axis runs over, the one named last changes fastest.
Arguments:
- tokens: bfloat16 [4096, 8192], P('ctx', 'chan'), may hold values from -6 to 6
- in_base: bfloat16 [8192, 3, 4096], P('ctx', None, 'chan'), may hold values from -0.0625 to 0.0625
- in_task: bfloat16 [8192, 3, 4096], P('ctx', None, 'chan'), may hold values from -0.03125 to 0.03125
- feat_weight: float32 [7, 3, 4096], P(None, None, 'chan'), may hold values from -2 to 2
- filter_taps: float32 [128, 4096], P(None, 'chan'), may hold values from -0.5 to 0.5
- decay_rates: float32 [4096], P('chan'), may hold values from 0.002 to 0.08
- skip_gain: float32 [4096], P('chan'), may hold values from -1 to 1
- out_base: bfloat16 [4096, 8192], P('chan', 'ctx'), may hold values from -0.1875 to 0.1875
- out_task: bfloat16 [4096, 8192], P('chan', 'ctx'), may hold values from -0.046875 to 0.046875
Outputs:
- layer_out: bfloat16 [4096, 8192], P('ctx', 'chan')
All inputs are finite; a program needn't handle non-finite values.
Results may differ from a plain program's by a relative error of at most 0.0092.
Values may be sent and summed in bfloat16 or wider, within the bound.
A program may use at most 128 MiB of HBM per device.

v0:
```python
import jax
import jax.numpy as jnp
from jax import lax
from jax.sharding import PartitionSpec as P


def shifted(value, axis, by):
    size = lax.axis_size(axis)
    pairs = [(i, i + by) for i in range(size) if 0 <= i + by < size]
    return lax.ppermute(value, axis, pairs)


def featurize_valid(extended, feat_weight, count):
    taps_short = feat_weight.shape[0]
    result = jnp.zeros((count,) + extended.shape[1:], jnp.float32)
    for offset in range(taps_short):
        begin_at = taps_short - 1 - offset
        result = result + feat_weight[offset] * extended[begin_at : begin_at + count].astype(
            jnp.float32
        )
    return result


def negate_task(base_part, task_part):
    return (base_part.astype(jnp.float32) - task_part.astype(jnp.float32)).astype(jnp.bfloat16)


def shards(
    tokens, in_base, in_task, feat_weight, filter_taps, decay_rates, skip_gain, out_base, out_task
):
    base_all, task_all = (
        lax.all_gather(in_base, "ctx", axis=0, tiled=True),
        lax.all_gather(in_task, "ctx", axis=0, tiled=True),
    )
    in_weight = negate_task(base_all, task_all)
    width_all = in_weight.shape[0]
    chan_local = in_weight.shape[2]
    flat_weight = in_weight.reshape(width_all, 3 * chan_local)
    tok_rows = tokens.shape[0]
    projected = jnp.dot(
        lax.all_gather(tokens, "chan", axis=1, tiled=True),
        flat_weight,
        preferred_element_type=jnp.float32,
    )
    projected = projected.astype(jnp.bfloat16).reshape(tok_rows, 3, chan_local)
    taps_long = filter_taps.shape[0]
    taps_short = feat_weight.shape[0]
    lag_values = jnp.arange(taps_long, dtype=jnp.float32)
    filter_full = filter_taps * jnp.exp(-decay_rates[None, :] * lag_values[:, None])
    rim_rows = shifted(projected[tok_rows - (taps_short - 1) :], "ctx", 1)
    extended = jnp.concatenate([rim_rows, projected], axis=0)
    featured = featurize_valid(extended, feat_weight, tok_rows)
    query_part = featured[:, 0, :]
    own_input = featured[:, 1, :] * featured[:, 2, :]
    input_rim = shifted(own_input[tok_rows - (taps_long - 1) :], "ctx", 1)
    long_input = jnp.concatenate([input_rim, own_input], axis=0)
    mixed = skip_gain * own_input
    conv_sum = jnp.zeros((tok_rows, chan_local), jnp.float32)
    for lag_index in range(taps_long):
        begin_at = taps_long - 1 - lag_index
        conv_sum = conv_sum + filter_full[lag_index] * long_input[begin_at : begin_at + tok_rows]
    mixed = mixed + conv_sum
    gated_out = (query_part * mixed).astype(jnp.bfloat16)
    base_cols, task_cols = (
        lax.all_gather(out_base, "ctx", axis=1, tiled=True),
        lax.all_gather(out_task, "ctx", axis=1, tiled=True),
    )
    out_weight = negate_task(base_cols, task_cols)
    partial_terms = jnp.dot(gated_out, out_weight, preferred_element_type=jnp.float32)
    summed = lax.psum_scatter(partial_terms, "chan", scatter_dimension=1, tiled=True)
    return summed.astype(jnp.bfloat16)


def solution(mesh):
    in_specs = (
        P("ctx", "chan"),
        P("ctx", None, "chan"),
        P("ctx", None, "chan"),
        P(None, None, "chan"),
        P(None, "chan"),
        P("chan"),
        P("chan"),
        P("chan", "ctx"),
        P("chan", "ctx"),
    )
    out_specs = P("ctx", "chan")
    return jax.shard_map(shards, mesh=mesh, in_specs=in_specs, out_specs=out_specs, check_vma=False)
```

profile of v0, /device:TPU:4, one launch (start us, length us, event | category | flops | bytes accessed | tf_op | source)
XLA Modules:
  0.0 755.3 jit_solution(2563523671187403728)
XLA Ops:
  6.5 0.0 all-gather.6.cloned.1.call-start
  6.5 2.3 copy.10
  8.8 0.0 all-gather.6.cloned.1.call-update
  8.9 0.0 all-gather.8.cloned.1.call-start
  8.9 2.3 copy.11
  11.2 0.0 all-gather.8.cloned.1.call-update
  11.3 0.0 all-gather.10.cloned.1.call-start
  11.3 0.7 all-gather.10.cloned.1.call-update
  12.0 0.0 all-gather.12.cloned.1.call-start
  12.0 0.5 all-gather.12.cloned.1.call-update
  12.6 0.0 all-gather.14.cloned.1.call-start
  12.6 0.5 all-gather.14.cloned.1.call-update
  13.2 0.0 reduce-scatter.2.cloned.1.call-start
  13.2 0.7 neg.4
  13.9 0.9 exponential_multiply_fusion
  14.9 1.0 fusion.391
  15.9 127.7 %all-gather.6.cloned.1.call-done = bf16[8192,3,128]{0,2,1:T(8,128)(2,1)} async-done(((bf16[1024,3,128]{0,2,1:T(8,128)(2,1)}), bf16[8192,3,128]{0,2,1:T(8,128)(2,1)}) %all-gather.6.cloned.1.call-update) | async-done | bytes 6291472 | tf_op jit(solution)/shard_map/all_gather | solution.py:32
  143.6 134.7 %all-gather.8.cloned.1.call-done = bf16[8192,3,128]{0,2,1:T(8,128)(2,1)} async-done(((bf16[1024,3,128]{0,2,1:T(8,128)(2,1)}), bf16[8192,3,128]{0,2,1:T(8,128)(2,1)}) %all-gather.8.cloned.1.call-update) | async-done | bytes 6291472 | tf_op jit(solution)/shard_map/all_gather | solution.py:33
  278.4 9.9 %subtract_convert_fusion = bf16[8192,3,128]{0,2,1:T(8,128)(2,1)} fusion(bf16[8192,3,128]{0,2,1:T(8,128)(2,1)} %all-gather.8.cloned.1.call-done, bf16[8192,3,128]{0,2,1:T(8,128)(2,1)} %all-gather.6.cloned.1.call-done), kind=kLoop, calls=%fused_computation.126 | loop fusion | flops 12582912 | bytes 18874368 | tf_op jit(solution)/shard_map/convert_element_type | solution.py:25
  288.3 102.3 %all-gather.10.cloned.1.call-done = bf16[512,8192]{1,0:T(8,128)(2,1)} async-done(((bf16[512,256]{1,0:T(8,128)(2,1)}), bf16[512,8192]{1,0:T(8,128)(2,1)}) %all-gather.10.cloned.1.call-update) | async-done | bytes 8388624 | tf_op jit(solution)/shard_map/all_gather | solution.py:41
  390.5 0.0 copy-start
  390.5 8.6 %convolution_convert_fusion = bf16[384,512]{1,0:T(8,128)(2,1)S(1)} fusion(bf16[8192,384]{0,1:T(8,128)(2,1)} %bitcast.287, bf16[512,8192]{1,0:T(8,128)(2,1)} %all-gather.10.cloned.1.call-done), kind=kOutput, calls=%fused_computation.255 | convolution fusion | flops 3221422080 | bytes 15073280 | tf_op jit(solution)/shard_map/dot_general | solution.py:40
  399.2 0.1 slice.1100
  399.3 2.5 collective-permute-start
  401.8 6.1 collective-permute-done
  407.9 1.5 multiply_add_fusion
  409.4 0.1 slice_bitcast_fusion.1
  409.5 4.6 collective-permute-start.1
  414.1 32.5 %all-gather.12.cloned.1.call-done = bf16[128,8192]{1,0:T(8,128)(2,1)} async-done(((bf16[128,1024]{1,0:T(8,128)(2,1)}), bf16[128,8192]{1,0:T(8,128)(2,1)}) %all-gather.12.cloned.1.call-update) | async-done | bytes 2097168 | tf_op jit(solution)/shard_map/all_gather | solution.py:65
  446.6 55.2 %all-gather.14.cloned.1.call-done = bf16[128,8192]{1,0:T(8,128)(2,1)} async-done(((bf16[128,1024]{1,0:T(8,128)(2,1)}), bf16[128,8192]{1,0:T(8,128)(2,1)}) %all-gather.14.cloned.1.call-update) | async-done | bytes 2097168 | tf_op jit(solution)/shard_map/all_gather | solution.py:66
  501.8 0.0 collective-permute-done.1
  501.8 0.0 copy-done
  501.8 23.9 %fusion = f32[512,8192]{1,0:T(8,128)} fusion(bf16[128,8192]{1,0:T(8,128)(2,1)} %all-gather.14.cloned.1.call-done, bf16[128,8192]{1,0:T(8,128)(2,1)} %all-gather.12.cloned.1.call-done, f32[512,128]{0,1:T(8,128)S(1)} %fusion.394, f32[127,128]{0,1:T(8,128)S(1)} %collective-permute-done.1, f32[512,3,128]{0,2,1:T(8,128)S(1)} %multiply_add_fusion, ...), kind=kOutput, calls=%fused_computation.128 | convolution fusion | flops 1103233024 | bytes 21627392 | tf_op jit(solution)/shard_map/dot_general | solution.py:69
  525.7 0.0 reduce-scatter.2.cloned.1.call-update
  525.7 221.0 %reduce-scatter.2.cloned.1.call-done = f32[512,256]{1,0:T(8,128)} async-done(((f32[512,8192]{1,0:T(8,128)}), f32[512,256]{1,0:T(8,128)}) %reduce-scatter.2.cloned.1.call-update) | async-done | bytes 524304 | tf_op jit(solution)/shard_map/reduce_scatter | solution.py:70
  746.7 1.8 convert_element_type.67
  (13 shorter events, 0.2 us)
Async XLA Ops:
  6.5 137.1 %all-gather.6.cloned.1.call-start = ((), (), s32[]{:S(2)}) async-start(), calls=%async_computation.1 | async-start | bytes 7077888 | tf_op jit(solution)/shard_map/all_gather | solution.py:32
  8.9 269.5 %all-gather.8.cloned.1.call-start = ((), (), s32[]{:S(2)}) async-start(), calls=%async_computation.2 | async-start | bytes 7077888 | tf_op jit(solution)/shard_map/all_gather | solution.py:33
  11.3 379.3 %all-gather.10.cloned.1.call-start = ((), (), s32[]{:S(2)}) async-start(), calls=%async_computation.3 | async-start | bytes 8650752 | tf_op jit(solution)/shard_map/all_gather | solution.py:41
  12.0 434.6 %all-gather.12.cloned.1.call-start = ((), (), s32[]{:S(2)}) async-start(), calls=%async_computation.4 | async-start | bytes 2359296 | tf_op jit(solution)/shard_map/all_gather | solution.py:65
  12.6 489.2 %all-gather.14.cloned.1.call-start = ((), (), s32[]{:S(2)}) async-start(), calls=%async_computation.5 | async-start | bytes 2359296 | tf_op jit(solution)/shard_map/all_gather | solution.py:66
  13.2 733.5 %reduce-scatter.2.cloned.1.call-start = ((), (), s32[]{:S(2)}) async-start(), calls=%async_computation.6 | async-start | bytes 17301504 | tf_op jit(solution)/shard_map/reduce_scatter | solution.py:70
  390.5 111.3 %copy-start = (f32[128]{0:T(128)S(1)}, f32[128]{0:T(128)}, u32[]{:S(2)}) copy-start(f32[128]{0:T(128)} %param.15) | copy-start | bytes 1540
  399.3 8.6 %collective-permute-start = (bf16[6,3,128]{0,2,1:T(8,128)(2,1)S(1)}, bf16[6,3,128]{0,2,1:T(8,128)(2,1)S(1)}, u32[]{:S(2)}, u32[]{:S(2)}) collective-permute-start(bf16[6,3,128]{0,2,1:T(8,128)(2,1)S(1)} %bitcast.290), channel_id=1, source_target_pairs={{0,32},{32,64},{64,96},{96,128},{128,160},{160,192},{192,224},{1,3... | collective-permute-start | bytes 13832 | tf_op jit(solution)/shard_map/ppermute | solution.py:10
  409.5 92.3 %collective-permute-start.1 = (f32[127,128]{0,1:T(8,128)S(1)}, f32[127,128]{0,1:T(8,128)S(1)}, u32[]{:S(2)}, u32[]{:S(2)}) collective-permute-start(f32[127,128]{0,1:T(8,128)S(1)} %slice_bitcast_fusion.1), channel_id=1, source_target_pairs={{0,32},{32,64},{64,96},{96,128},{128,160},{160,192},{192,224},{1,3... | collective-permute-start | bytes 195080 | tf_op jit(solution)/shard_map/ppermute | solution.py:10
Sparse Core Ops, SparseCore 0:
  9.1 134.4 all-gather.5
  145.4 132.9 all-gather.7
  280.9 109.5 all-gather.9
  392.2 54.3 all-gather.11
  448.2 53.5 all-gather.13
  525.8 220.7 reduce-scatter.1
where the time goes:
time: 756 us; the launch traced here: 755 us
  waiting for transfers between devices  681 us (90%)
  matrix products  32.5 us (4%)
  other arithmetic  14.8 us (2%)
  between operations  13.6 us (2%)
    reduce_scatter x1, waiting for transfers between devices, shards(): lax.psum_scatter(partial_terms, 'chan', scatter_dimension=1, tiled=True)  221 us
    all_gather x1, waiting for transfers between devices, shards(): lax.all_gather(in_task, 'ctx', axis=0, tiled=True)  135 us
    all_gather x1, waiting for transfers between devices, shards(): lax.all_gather(in_base, 'ctx', axis=0, tiled=True)  128 us
    all_gather x1, waiting for transfers between devices, shards(): lax.all_gather(tokens, 'chan', axis=1, tiled=True)  102 us
    all_gather x1, waiting for transfers between devices, shards(): lax.all_gather(out_task, 'ctx', axis=1, tiled=True)  55.2 us
    all_gather x1, waiting for transfers between devices, shards(): lax.all_gather(out_base, 'ctx', axis=1, tiled=True)  32.5 us
    dot_general x1, matrix products, shards(): jnp.dot(gated_out, out_weight, preferred_element_type=jnp.float32)  23.9 us
  transfers between devices with their start and end apart: 8, of which 7 were waited for; matrix products, arithmetic and copies ran while one was open for 3% of the time, Pallas kernels for 0%

commit v1 on v0

--- a/solution.py
+++ b/solution.py
@@ -28,10 +28,15 @@
 def shards(
     tokens, in_base, in_task, feat_weight, filter_taps, decay_rates, skip_gain, out_base, out_task
 ):
-    base_all, task_all = (
-        lax.all_gather(in_base, "ctx", axis=0, tiled=True),
-        lax.all_gather(in_task, "ctx", axis=0, tiled=True),
-    )
+
+    def begin_floor(q_in, mesh_dim="ctx"):
+        r_now = tuple((q_in for _ in range(lax.axis_size(mesh_dim))))
+        formed = jnp.stack(r_now)
+        local_now = lax.all_to_all(formed, axis_name=mesh_dim, split_axis=0, concat_axis=0)
+        local_out = jnp.concatenate(local_now, axis=0)
+        return local_out
+
+    base_all, task_all = (begin_floor(in_base), lax.all_gather(in_task, "ctx", axis=0, tiled=True))
     in_weight = negate_task(base_all, task_all)
     width_all = in_weight.shape[0]
     chan_local = in_weight.shape[2]

time: 756 us -> 688 us (0.910)
  waiting for transfers between devices: 681 us -> 585 us
  local copies, waits for them, and re-layouts: 5.88 us -> 19.2 us
  other arithmetic: 14.8 us -> 23.3 us
    all_gather x1 -> x0, waiting for transfers between devices: 128 us -> none  [shards(): lax.all_gather(in_base, 'ctx', axis=0, tiled=True)]
    all_to_all x0 -> x1, waiting for transfers between devices: none -> 107 us  [begin_floor(): lax.all_to_all(formed, axis_name=mesh_dim, split_axis=0, concat_axis=0)]
    all_gather x1, waiting for transfers between devices: 135 us -> 57.6 us  [shards(): lax.all_gather(in_task, 'ctx', axis=0, tiled=True)]
    all_gather x1, waiting for transfers between devices: 32.5 us -> 55.4 us  [shards(): lax.all_gather(out_base, 'ctx', axis=1, tiled=True)]
    all_gather x1, waiting for transfers between devices: 55.2 us -> 32.5 us  [shards(): lax.all_gather(out_task, 'ctx', axis=1, tiled=True)]
    convert_element_type x0 -> x1, local copies, waits for them, and re-layouts: none -> 11.8 us  [negate_task(): base_part.astype(jnp.float32) - task_part.astype(jnp.float32)]
    unnamed x0 -> x1, other arithmetic: none -> 8.94 us
  transfers between devices with their start and end apart: 8 -> 8, of which waited for: 7 -> 7; matrix products, arithmetic and copies ran while one was open for 3% -> 7% of each run, Pallas kernels for 0% -> 0%
where the time goes in v1:
time: 688 us; the launch traced here: 687 us
  waiting for transfers between devices  585 us (85%)
  matrix products  32.5 us (5%)
  other arithmetic  23.3 us (3%)
  local copies, waits for them, and re-layouts  19.2 us (3%)
  starting transfers between devices  14.2 us (2%)
  between operations  13.3 us (2%)
    reduce_scatter x1, waiting for transfers between devices, shards(): lax.psum_scatter(partial_terms, 'chan', scatter_dimension=1, tiled=True)  221 us
    all_to_all x1, waiting for transfers between devices, begin_floor(): lax.all_to_all(formed, axis_name=mesh_dim, split_axis=0, concat_axis=0)  107 us
    all_gather x1, waiting for transfers between devices, shards(): lax.all_gather(tokens, 'chan', axis=1, tiled=True)  103 us
    all_gather x1, waiting for transfers between devices, shards(): lax.all_gather(in_task, 'ctx', axis=0, tiled=True)  57.6 us
    all_gather x1, waiting for transfers between devices, shards(): lax.all_gather(out_base, 'ctx', axis=1, tiled=True)  55.4 us
    all_gather x1, waiting for transfers between devices, shards(): lax.all_gather(out_task, 'ctx', axis=1, tiled=True)  32.5 us
    dot_general x1, matrix products, shards(): jnp.dot(gated_out, out_weight, preferred_element_type=jnp.float32)  23.9 us
  transfers between devices with their start and end apart: 8, of which 7 were waited for; matrix products, arithmetic and copies ran while one was open for 7% of the time, Pallas kernels for 0%

profile of v1, /device:TPU:4, one launch (start us, length us, event | category | flops | bytes accessed | tf_op | source)
XLA Modules:
  0.0 687.4 jit_solution(3188731824433206268)
XLA Ops:
  6.5 0.0 all-gather.5.cloned.1.call-start
  6.5 2.3 copy.14
  8.8 0.0 all-gather.5.cloned.1.call-update
  8.8 0.0 all-gather.7.cloned.1.call-start
  8.9 0.7 all-gather.7.cloned.1.call-update
  9.6 0.0 all-gather.11.cloned.1.call-start
  9.6 0.7 all-gather.11.cloned.1.call-update
  10.3 1.4 copy.12
  11.7 3.4 stack.2
  15.2 0.0 copy-start.2
  15.2 0.0 copy-start.1
  15.2 0.0 copy-start
  15.2 7.0 %all-to-all-start = ((bf16[8,1024,3,128]{1,3,2,0:T(8,128)(2,1)}), bf16[8,1024,3,128]{1,3,2,0:T(8,128)(2,1)}, u32[]{:S(2)}, u32[]{:S(2)}) async-start(bf16[8,1024,3,128]{1,3,2,0:T(8,128)(2,1)} %stack.2), calls=%async_computation | async-start | bytes 12582912 | tf_op jit(solution)/shard_map/all_to_all | solution.py:35
  22.2 0.0 all-gather.9.cloned.1.call-start
  22.2 0.6 all-gather.9.cloned.1.call-update
  22.7 0.0 reduce-scatter.2.cloned.1.call-start
  22.8 0.0 copy-done.2
  22.8 0.0 copy-done.1
  22.9 0.0 copy-done
  23.1 107.4 %all-to-all-done = bf16[8,1024,3,128]{1,3,2,0:T(8,128)(2,1)} async-done(((bf16[8,1024,3,128]{1,3,2,0:T(8,128)(2,1)}), bf16[8,1024,3,128]{1,3,2,0:T(8,128)(2,1)}, u32[]{:S(2)}, u32[]{:S(2)}) %all-to-all-start) | async-done | bytes 6291488 | tf_op jit(solution)/shard_map/all_to_all | solution.py:35
  130.4 8.9 %convert_bitcast_fusion = f32[8,3,16,8,1024]{4,3,2,1,0:T(8,128)} fusion(bf16[8,1024,3,128]{1,3,2,0:T(8,128)(2,1)} %all-to-all-done), kind=kLoop, calls=%fused_computation.126 | loop fusion | flops 3145728 | bytes 18874368
  139.4 11.8 %copy.22 = f32[8,3,16,8,1024]{4,3,0,2,1:T(8,128)} copy(f32[8,3,16,8,1024]{4,3,2,1,0:T(8,128)} %convert_bitcast_fusion) | data formatting | bytes 25165824 | tf_op jit(solution)/shard_map/convert_element_type | solution.py:25
  151.2 57.6 %all-gather.5.cloned.1.call-done = bf16[8192,3,128]{0,2,1:T(8,128)(2,1)} async-done(((bf16[1024,3,128]{0,2,1:T(8,128)(2,1)}), bf16[8192,3,128]{0,2,1:T(8,128)(2,1)}) %all-gather.5.cloned.1.call-update) | async-done | bytes 6291472 | tf_op jit(solution)/shard_map/all_gather | solution.py:39
  208.9 11.0 %subtract_convert_fusion = bf16[8192,3,128]{0,2,1:T(8,128)(2,1)} fusion(f32[8192,3,128]{0,2,1:T(8,128)} %bitcast.290, bf16[8192,3,128]{0,2,1:T(8,128)(2,1)} %all-gather.5.cloned.1.call-done), kind=kLoop, calls=%fused_computation.127 | loop fusion | flops 9437184 | bytes 25165824 | tf_op jit(solution)/shard_map/convert_element_type | solution.py:25
  219.8 102.8 %all-gather.7.cloned.1.call-done = bf16[512,8192]{1,0:T(8,128)(2,1)} async-done(((bf16[512,256]{1,0:T(8,128)(2,1)}), bf16[512,8192]{1,0:T(8,128)(2,1)}) %all-gather.7.cloned.1.call-update) | async-done | bytes 8388624 | tf_op jit(solution)/shard_map/all_gather | solution.py:46
  322.6 0.0 copy-start.3
  322.6 8.6 %convolution_convert_fusion = bf16[384,512]{1,0:T(8,128)(2,1)S(1)} fusion(bf16[8192,384]{0,1:T(8,128)(2,1)} %bitcast.291, bf16[512,8192]{1,0:T(8,128)(2,1)} %all-gather.7.cloned.1.call-done), kind=kOutput, calls=%fused_computation.256 | convolution fusion | flops 3221422080 | bytes 15073280 | tf_op jit(solution)/shard_map/dot_general | solution.py:45
  331.3 0.1 slice.1100
  331.4 2.5 collective-permute-start
  333.9 6.2 collective-permute-done
  340.1 1.5 multiply_add_fusion
  341.6 0.1 slice_bitcast_fusion.1
  341.7 4.6 collective-permute-start.1
  346.3 32.5 %all-gather.11.cloned.1.call-done = bf16[128,8192]{1,0:T(8,128)(2,1)} async-done(((bf16[128,1024]{1,0:T(8,128)(2,1)}), bf16[128,8192]{1,0:T(8,128)(2,1)}) %all-gather.11.cloned.1.call-update) | async-done | bytes 2097168 | tf_op jit(solution)/shard_map/all_gather | solution.py:71
  378.8 55.4 %all-gather.9.cloned.1.call-done = bf16[128,8192]{1,0:T(8,128)(2,1)} async-done(((bf16[128,1024]{1,0:T(8,128)(2,1)}), bf16[128,8192]{1,0:T(8,128)(2,1)}) %all-gather.9.cloned.1.call-update) | async-done | bytes 2097168 | tf_op jit(solution)/shard_map/all_gather | solution.py:70
  434.2 0.0 collective-permute-done.1
  434.2 0.0 copy-done.3
  434.2 23.9 %fusion = f32[512,8192]{1,0:T(8,128)} fusion(bf16[128,8192]{1,0:T(8,128)(2,1)} %all-gather.11.cloned.1.call-done, bf16[128,8192]{1,0:T(8,128)(2,1)} %all-gather.9.cloned.1.call-done, f32[512,128]{0,1:T(8,128)S(1)} %fusion.394, f32[127,128]{0,1:T(8,128)S(1)} %collective-permute-done.1, f32[512,3,128]{0,2,1:T(8,128)S(1)} %multiply_add_fusion, ...), kind=kOutput, calls=%fused_computation.129 | convolution fusion | flops 1103233024 | bytes 21627392 | tf_op jit(solution)/shard_map/dot_general | solution.py:74
  458.1 0.0 reduce-scatter.2.cloned.1.call-update
  458.1 220.9 %reduce-scatter.2.cloned.1.call-done = f32[512,256]{1,0:T(8,128)} async-done(((f32[512,8192]{1,0:T(8,128)}), f32[512,256]{1,0:T(8,128)}) %reduce-scatter.2.cloned.1.call-update) | async-done | bytes 524304 | tf_op jit(solution)/shard_map/reduce_scatter | solution.py:75
  679.1 1.8 convert_element_type.71
  (16 shorter events, 0.2 us)
Async XLA Ops:
  6.5 202.3 %all-gather.5.cloned.1.call-start = ((), (), s32[]{:S(2)}) async-start(), calls=%async_computation.2 | async-start | bytes 7077888 | tf_op jit(solution)/shard_map/all_gather | solution.py:39
  8.8 313.8 %all-gather.7.cloned.1.call-start = ((), (), s32[]{:S(2)}) async-start(), calls=%async_computation.3 | async-start | bytes 8650752 | tf_op jit(solution)/shard_map/all_gather | solution.py:46
  9.6 369.3 %all-gather.11.cloned.1.call-start = ((), (), s32[]{:S(2)}) async-start(), calls=%async_computation.5 | async-start | bytes 2359296 | tf_op jit(solution)/shard_map/all_gather | solution.py:71
  15.2 7.6 %copy-start.2 = (f32[128]{0:T(128)S(1)}, f32[128]{0:T(128)}, u32[]{:S(2)}) copy-start(f32[128]{0:T(128)} %param.14) | copy-start | bytes 1540
  15.2 7.6 %copy-start.1 = (f32[7,3,128]{2,0,1:T(8,128)S(1)}, f32[7,3,128]{2,0,1:T(8,128)}, u32[]{:S(2)}) copy-start(f32[7,3,128]{2,0,1:T(8,128)} %param.12) | copy-start | bytes 32260
  15.2 7.7 %copy-start = (f32[128,128]{1,0:T(8,128)S(1)}, f32[128,128]{1,0:T(8,128)}, u32[]{:S(2)}) copy-start(f32[128,128]{1,0:T(8,128)} %param.13) | copy-start | bytes 196612
  15.2 115.3 %all-to-all-start = ((bf16[8,1024,3,128]{1,3,2,0:T(8,128)(2,1)}), bf16[8,1024,3,128]{1,3,2,0:T(8,128)(2,1)}, u32[]{:S(2)}, u32[]{:S(2)}) async-start(bf16[8,1024,3,128]{1,3,2,0:T(8,128)(2,1)} %stack.2), calls=%async_computation | async-start | bytes 12582912 | tf_op jit(solution)/shard_map/all_to_all | solution.py:35
  22.2 412.0 %all-gather.9.cloned.1.call-start = ((), (), s32[]{:S(2)}) async-start(), calls=%async_computation.4 | async-start | bytes 2359296 | tf_op jit(solution)/shard_map/all_gather | solution.py:70
  22.7 656.3 %reduce-scatter.2.cloned.1.call-start = ((), (), s32[]{:S(2)}) async-start(), calls=%async_computation.6 | async-start | bytes 17301504 | tf_op jit(solution)/shard_map/reduce_scatter | solution.py:75
  322.6 111.6 %copy-start.3 = (f32[128]{0:T(128)S(1)}, f32[128]{0:T(128)}, u32[]{:S(2)}) copy-start(f32[128]{0:T(128)} %param.15) | copy-start | bytes 1540
  331.4 8.7 %collective-permute-start = (bf16[6,3,128]{0,2,1:T(8,128)(2,1)S(1)}, bf16[6,3,128]{0,2,1:T(8,128)(2,1)S(1)}, u32[]{:S(2)}, u32[]{:S(2)}) collective-permute-start(bf16[6,3,128]{0,2,1:T(8,128)(2,1)S(1)} %bitcast.294), channel_id=1, source_target_pairs={{0,32},{32,64},{64,96},{96,128},{128,160},{160,192},{192,224},{1,3... | collective-permute-start | bytes 13832 | tf_op jit(solution)/shard_map/ppermute | solution.py:10
  341.7 92.5 %collective-permute-start.1 = (f32[127,128]{0,1:T(8,128)S(1)}, f32[127,128]{0,1:T(8,128)S(1)}, u32[]{:S(2)}, u32[]{:S(2)}) collective-permute-start(f32[127,128]{0,1:T(8,128)S(1)} %slice_bitcast_fusion.1), channel_id=1, source_target_pairs={{0,32},{32,64},{64,96},{96,128},{128,160},{160,192},{192,224},{1,3... | collective-permute-start | bytes 195080 | tf_op jit(solution)/shard_map/ppermute | solution.py:10
Sparse Core Ops, SparseCore 0:
  9.1 199.6 all-gather.4
  211.4 111.1 all-gather.6
  324.4 54.3 all-gather.10
  380.5 53.6 all-gather.8
  458.3 220.7 reduce-scatter.1
